TPU v7x, 256 devices: a whole 4x4x8 slice. The times are simulated.
256 devices in a mesh: pop: 32 (over x, y, core), site: 8 (over z).
Axes of the slice: x: 4, y: 4, z: 8, core: 2. Of those that a mesh axis runs over, the one named last changes fastest.
Arguments:
- profile: bfloat16 [32768, 96], P(('pop', 'site')), may hold values from 0 to 1
- panel: bfloat16 [32768, 128], P(('pop', 'site')), may hold values from -6 to 6
- visit_person: int32 [131072], P(('pop', 'site')), may hold values from 0 to 127
- visit_owner: int32 [131072], P(('pop', 'site')), may hold values from 0 to 31, as said below
- visit_row: int32 [131072], P(('pop', 'site')), may hold values from 0 to 1023, as said below
- visit_start: int32 [131072], P(('pop', 'site')), may hold values from 0 to 95
- visit_length: int32 [131072], P(('pop', 'site')), may hold values from 2 to 48
- tile_loc: int32 [2048], P(('pop', 'site')), may hold values from 0 to 7
Outputs:
- exposure: bfloat16 [32768, 128], P(('pop', 'site'))
Inputs may be any that keep to these rules, and one draw needn't show every extreme that they name: `visit_owner`: all devices with one site index send the same number of visits to a given owner index; at most 24 visits of one device go to one owner index, and in every draw some owner index receives exactly 24 from every device of a site index. `visit_row`: among the visits that reach one owner device the rows are distinct; in each tile the rows that are used come first and the rest are empty.
All inputs are finite; a program needn't handle non-finite values.
Results may differ from a plain program's by a relative error of at most 0.013.
Values may be sent and summed in bfloat16 or wider, within the bound.
No kernel may reach another device: no remote copies, remote signals or barrier semaphores. Data moves between devices by JAX's collectives and lax.ppermute only.
A program may use at most 64 MiB of HBM per device.

v0:
```python
import math
import jax
import jax.numpy as jnp
from jax import lax
from jax.sharding import PartitionSpec as P


def pair_terms(own_weights, own_places, running, pieces):
    far_weights, far_panel, far_places = pieces
    piece_tiles = far_weights.shape[0]
    group_size = math.gcd(piece_tiles, 8)
    group_count = piece_tiles // group_size
    grouped = (
        far_weights.reshape((group_count, group_size) + far_weights.shape[1:]),
        far_panel.reshape((group_count, group_size) + far_panel.shape[1:]),
        far_places.reshape(group_count, group_size),
    )

    def one_group(carried, item):
        group_weights, group_panel, group_places = item
        same_place = (own_places[:, None] == group_places[None, :]).astype(jnp.bfloat16)
        masked_far = group_weights[None, :, :, :] * same_place[:, :, None, None]
        copresence = jnp.einsum(
            "ars,abqs->abrq", own_weights, masked_far, preferred_element_type=jnp.float32
        )
        high_part = copresence.astype(jnp.bfloat16)
        low_part = (copresence - high_part.astype(jnp.float32)).astype(jnp.bfloat16)
        added = jnp.einsum(
            "abrq,bqc->arc", high_part, group_panel, preferred_element_type=jnp.float32
        )
        added = added + jnp.einsum(
            "abrq,bqc->arc", low_part, group_panel, preferred_element_type=jnp.float32
        )
        return (carried + added, None)

    result_sum, unused = lax.scan(one_group, running, grouped)
    return result_sum


def per_device(
    profile, panel, visit_person, visit_owner, visit_row, visit_start, visit_length, tile_loc
):
    pop_count = lax.axis_size("pop")
    visit_count = visit_person.shape[0]
    person_count, slot_count = profile.shape
    panel_width = panel.shape[1]
    capacity = visit_count // pop_count * 3 // 2
    tile_count = tile_loc.shape[0]
    row_count = tile_count * 128
    slot_ids = jnp.arange(slot_count, dtype=jnp.int32)
    finish = jnp.minimum(visit_start + visit_length, slot_count)
    inside = (slot_ids[None, :] >= visit_start[:, None]) & (slot_ids[None, :] < finish[:, None])
    weights = jnp.where(inside, profile[visit_person], jnp.zeros((), jnp.bfloat16))
    visit_panel = panel[visit_person]
    owner_hot = (visit_owner[:, None] == jnp.arange(pop_count, dtype=jnp.int32)[None, :]).astype(
        jnp.int32
    )
    position = jnp.sum((jnp.cumsum(owner_hot, axis=0) - 1) * owner_hot, axis=1)
    send_index = visit_owner * capacity + position
    send_weights = (
        jnp.zeros((pop_count * capacity, slot_count), jnp.bfloat16)
        .at[send_index]
        .set(weights)
        .reshape(pop_count, capacity, slot_count)
    )
    send_panel = (
        jnp.zeros((pop_count * capacity, panel_width), jnp.bfloat16)
        .at[send_index]
        .set(visit_panel)
        .reshape(pop_count, capacity, panel_width)
    )
    send_rows = (
        jnp.full((pop_count * capacity,), row_count, jnp.int32)
        .at[send_index]
        .set(visit_row)
        .reshape(pop_count, capacity)
    )
    got_weights, got_panel, got_rows = (
        lax.all_to_all(send_weights, "pop", split_axis=0, concat_axis=0, tiled=True),
        lax.all_to_all(send_panel, "pop", split_axis=0, concat_axis=0, tiled=True),
        lax.all_to_all(send_rows, "pop", split_axis=0, concat_axis=0, tiled=True),
    )
    target = got_rows.reshape(-1)
    tile_weights = (
        jnp.zeros((row_count, slot_count), jnp.bfloat16)
        .at[target]
        .set(got_weights.reshape(-1, slot_count), mode="drop")
        .reshape(tile_count, 128, slot_count)
    )
    tile_panel = (
        jnp.zeros((row_count, panel_width), jnp.bfloat16)
        .at[target]
        .set(got_panel.reshape(-1, panel_width), mode="drop")
        .reshape(tile_count, 128, panel_width)
    )
    initial = jnp.zeros((tile_count, 128, panel_width), jnp.float32)
    summed_rows = pair_terms(
        tile_weights,
        tile_loc,
        initial,
        (
            lax.all_gather(tile_weights, "site", axis=0, tiled=True),
            lax.all_gather(tile_panel, "site", axis=0, tiled=True),
            lax.all_gather(tile_loc, "site", axis=0, tiled=True),
        ),
    )
    row_result = (summed_rows / slot_count).astype(jnp.bfloat16).reshape(row_count, panel_width)
    sent_back = row_result[jnp.minimum(got_rows, row_count - 1)]
    returned = lax.all_to_all(sent_back, "pop", split_axis=0, concat_axis=0, tiled=True)
    own_results = returned.reshape(pop_count * capacity, panel_width)[send_index]
    person_hot = (
        jnp.arange(person_count, dtype=jnp.int32)[:, None] == visit_person[None, :]
    ).astype(jnp.bfloat16)
    return jnp.dot(person_hot, own_results, preferred_element_type=jnp.float32).astype(jnp.bfloat16)


def solution(mesh):
    placed = (
        P(("pop", "site"), None),
        P(("pop", "site"), None),
        P(("pop", "site")),
        P(("pop", "site")),
        P(("pop", "site")),
        P(("pop", "site")),
        P(("pop", "site")),
        P(("pop", "site")),
    )
    return jax.shard_map(
        per_device, mesh=mesh, in_specs=placed, out_specs=P(("pop", "site"), None), check_vma=False
    )
```

profile of v0, /device:TPU:1, one launch (start us, length us, event | category | flops | bytes accessed | tf_op | source)
XLA Modules:
  0.0 205.3 jit_solution(10561987336551839992)
XLA Ops:
  10.2 2.6 %scatter_custom_fusion = s32[768]{0:T(1024)S(1)} fusion(s32[512]{0:T(512)S(1)} %get-tuple-element.104, s32[512]{0:T(512)} %param.14, s32[]{:T(128)} %constant.8.clone.1), kind=kCustom, calls=%fused_computation.71 | custom fusion | bytes 3584 | tf_op jit(solution)/shard_map/scatter | solution.py:75
  13.5 8.6 %all-to-all-start = ((s32[32,1,24]{2,1,0:T(1,128)}), s32[32,1,24]{2,1,0:T(1,128)S(1)}, u32[]{:S(2)}, u32[]{:S(2)}) async-start(s32[32,1,24]{2,1,0:T(1,128)} %bitcast.2), calls=%async_computation | async-start | bytes 32768 | tf_op jit(solution)/shard_map/all_to_all | solution.py:81
  23.6 3.9 %scatter_custom_fusion.1 = bf16[768,96]{1,0:T(8,128)(2,1)} fusion(s32[512]{0:T(512)S(1)} %get-tuple-element.104, s32[512]{0:T(512)S(1)} %get-tuple-element.105, s32[512]{0:T(512)} %param.15, bf16[]{:T(256)} %constant.19.clone.1, bf16[128,96]{1,0:T(8,128)(2,1)S(1)} %copy.29, s32[1024]{0:T(1024)S(1)} %pad_clamp_fusion.2), kind=kCustom, calls=%fused_computation.40 | custom fusion | flops 196608 | bytes 189440 | tf_op jit(solution)/shard_map/scatter | solution.py:63
  28.9 6.0 %all-to-all-start.1 = ((bf16[32,24,96]{2,1,0:T(8,128)(2,1)}), bf16[32,24,96]{2,1,0:T(8,128)(2,1)S(1)}, u32[]{:S(2)}, u32[]{:S(2)}) async-start(bf16[32,24,96]{2,1,0:T(8,128)(2,1)} %bitcast.3), calls=%async_computation.1 | async-start | bytes 393216 | tf_op jit(solution)/shard_map/all_to_all | solution.py:79
  36.3 7.0 %all-to-all-done.1 = bf16[32,24,96]{2,1,0:T(8,128)(2,1)S(1)} async-done(((bf16[32,24,96]{2,1,0:T(8,128)(2,1)}), bf16[32,24,96]{2,1,0:T(8,128)(2,1)S(1)}, u32[]{:S(2)}, u32[]{:S(2)}) %all-to-all-start.1) | async-done | bytes 147488 | tf_op jit(solution)/shard_map/all_to_all | solution.py:79
  43.2 4.3 %scatter_custom_fusion.2 = bf16[1024,96]{1,0:T(8,128)(2,1)S(1)} fusion(s32[768]{0:T(1024)S(1)} %fusion.39, bf16[768,96]{1,0:T(8,128)(2,1)S(1)} %bitcast.114, bf16[]{:T(256)} %constant.19.clone.1), kind=kCustom, calls=%fused_computation.47 | custom fusion | bytes 196610 | tf_op jit(solution)/shard_map/scatter | solution.py:87
  48.5 3.0 %scatter_custom_fusion.3 = bf16[768,128]{1,0:T(8,128)(2,1)S(1)} fusion(s32[512]{0:T(512)S(1)} %get-tuple-element.104, bf16[128,128]{1,0:T(8,128)(2,1)S(1)} %copy-done, s32[1024]{0:T(1024)S(1)} %pad_clamp_fusion.2, bf16[]{:T(256)} %constant.19.clone.1), kind=kCustom, calls=%fused_computation.41 | custom fusion | bytes 196610 | tf_op jit(solution)/shard_map/scatter | solution.py:69
  51.5 11.9 %all_to_all.24 = bf16[32,24,128]{2,1,0:T(8,128)(2,1)S(1)} all-to-all(bf16[32,24,128]{2,1,0:T(8,128)(2,1)S(1)} %bitcast.112), channel_id=1, replica_groups=mesh['pop'=32,'site'=8] {'pop'}, dimensions={0} | all-to-all | bytes 393216 | tf_op jit(solution)/shard_map/all_to_all | solution.py:80
  63.4 4.9 %scatter_custom_fusion.4 = bf16[1024,128]{1,0:T(8,128)(2,1)} fusion(s32[768]{0:T(1024)S(1)} %fusion.39, bf16[768,128]{1,0:T(8,128)(2,1)S(1)} %bitcast.115, bf16[]{:T(256)} %constant.19.clone.1), kind=kCustom, calls=%fused_computation.43 | custom fusion | bytes 262146 | tf_op jit(solution)/shard_map/scatter | solution.py:93
  69.9 13.6 %all-reduce = s32[64]{0:T(128)S(1)} all-reduce(s32[64]{0:T(128)S(1)} %dynamic-update-slice), channel_id=1, replica_groups=mesh['pop'=32,'site'=8] {'site'}, use_global_device_ids=true, to_apply=%add | all-reduce | flops 64 | bytes 512
  83.9 3.5 %all-gather.3.cloned.1.call-done = bf16[64,128,96]{1,0,2:T(8,128)(2,1)} async-done(((bf16[8,128,96]{1,0,2:T(8,128)(2,1)}), bf16[64,128,96]{1,0,2:T(8,128)(2,1)}) %all-gather.3.cloned.1.call-update) | async-done | bytes 1572880 | tf_op jit(solution)/shard_map/all_gather | solution.py:102
  87.3 42.4 %all-gather.5.cloned.1.call-done = bf16[64,128,128]{2,1,0:T(8,128)(2,1)} async-done(((bf16[8,128,128]{2,1,0:T(8,128)(2,1)}), bf16[64,128,128]{2,1,0:T(8,128)(2,1)}) %all-gather.5.cloned.1.call-update) | async-done | bytes 2097168 | tf_op jit(solution)/shard_map/all_gather | solution.py:103
  129.7 44.4 %while.11 = (s32[]{:T(128)}, f32[8,128,128]{2,1,0:T(8,128)S(1)}, bf16[8,8,128,96]{2,1,0,3:T(8,128)(2,1)}, s32[8]{0:T(128)S(1)}, s32[8,8]{1,0:T(8,128)S(1)}, /*in...) while((s32[]{:T(128)}, f32[8,128,128]{2,1,0:T(8,128)S(1)}, ...), condition=%wide.region_9.10_spmd.clone, body=%wide.region_8.9_spmd.clone.sunk | while | flops 743571584 | bytes 16384511 | solution.py:36
  133.4 1.9 fusion.68
  139.0 1.9 fusion.68
  144.5 1.9 fusion.68
  150.1 1.9 fusion.68
  155.6 1.9 fusion.68
  161.2 1.9 fusion.68
  166.7 1.9 fusion.68
  172.3 1.9 fusion.68
  174.3 2.5 %gather_fusion = bf16[768,128]{1,0:T(8,128)(2,1)} fusion(bf16[1024,128]{1,0:T(8,128)(2,1)S(1)} %bitcast.106, s32[1024]{0:T(1024)S(1)} %pad_clamp_fusion.1), kind=kCustom, calls=%fused_computation.2 | custom fusion | bytes 396288 | tf_op jit(solution)/shard_map/gather | solution.py:108
  176.8 11.2 %all-to-all-start.3 = ((bf16[32,24,128]{2,1,0:T(8,128)(2,1)}), bf16[32,24,128]{2,1,0:T(8,128)(2,1)S(1)}, u32[]{:S(2)}, u32[]{:S(2)}) async-start(bf16[32,24,128]{2,1,0:T(8,128)(2,1)} %bitcast.14), calls=%async_computation.3 | async-start | bytes 393216 | tf_op jit(solution)/shard_map/all_to_all | solution.py:109
  188.0 8.3 %all-to-all-done.3 = bf16[32,24,128]{2,1,0:T(8,128)(2,1)S(1)} async-done(((bf16[32,24,128]{2,1,0:T(8,128)(2,1)}), bf16[32,24,128]{2,1,0:T(8,128)(2,1)S(1)}, u32[]{:S(2)}, u32[]{:S(2)}) %all-to-all-start.3) | async-done | bytes 196640 | tf_op jit(solution)/shard_map/all_to_all | solution.py:109
  (90 shorter events, 42.2 us)
Async XLA Ops:
  6.5 41.9 %copy-start = (bf16[128,128]{1,0:T(8,128)(2,1)S(1)}, bf16[128,128]{1,0:T(8,128)(2,1)}, u32[]{:S(2)}) copy-start(bf16[128,128]{1,0:T(8,128)(2,1)} %param.11) | copy-start | bytes 98308
  6.5 61.8 %copy-start.3 = (u32[256]{0:T(256)S(1)}, u32[256]{0:T(256)}, u32[]{:S(2)}) copy-start(u32[256]{0:T(256)} %constant.52) | copy-start | bytes 3076
  6.5 63.1 %copy-start.1 = (s32[8]{0:T(128)S(1)}, s32[8]{0:T(128)}, u32[]{:S(2)}) copy-start(s32[8]{0:T(128)} %param.17) | copy-start | bytes 100
  13.5 15.5 %all-to-all-start = ((s32[32,1,24]{2,1,0:T(1,128)}), s32[32,1,24]{2,1,0:T(1,128)S(1)}, u32[]{:S(2)}, u32[]{:S(2)}) async-start(s32[32,1,24]{2,1,0:T(1,128)} %bitcast.2), calls=%async_computation | async-start | bytes 32768 | tf_op jit(solution)/shard_map/all_to_all | solution.py:81
  28.9 14.3 %all-to-all-start.1 = ((bf16[32,24,96]{2,1,0:T(8,128)(2,1)}), bf16[32,24,96]{2,1,0:T(8,128)(2,1)S(1)}, u32[]{:S(2)}, u32[]{:S(2)}) async-start(bf16[32,24,96]{2,1,0:T(8,128)(2,1)} %bitcast.3), calls=%async_computation.1 | async-start | bytes 393216 | tf_op jit(solution)/shard_map/all_to_all | solution.py:79
  34.9 52.4 %all-gather.3.cloned.1.call-start = ((), (), s32[]{:S(2)}) async-start(), calls=%async_computation.4 | async-start | bytes 1769472 | tf_op jit(solution)/shard_map/all_gather | solution.py:102
  48.4 81.3 %all-gather.5.cloned.1.call-start = ((), (), s32[]{:S(2)}) async-start(), calls=%async_computation.5 | async-start | bytes 2359296 | tf_op jit(solution)/shard_map/all_gather | solution.py:103
  174.2 23.5 %copy-start.2 = (s32[512]{0:T(512)S(1)}, s32[512]{0:T(512)}, u32[]{:S(2)}) copy-start(s32[512]{0:T(512)} %param.12) | copy-start | bytes 6148
  176.8 19.6 %all-to-all-start.3 = ((bf16[32,24,128]{2,1,0:T(8,128)(2,1)}), bf16[32,24,128]{2,1,0:T(8,128)(2,1)S(1)}, u32[]{:S(2)}, u32[]{:S(2)}) async-start(bf16[32,24,128]{2,1,0:T(8,128)(2,1)} %bitcast.14), calls=%async_computation.3 | async-start | bytes 393216 | tf_op jit(solution)/shard_map/all_to_all | solution.py:109
Sparse Core Ops, SparseCore 0:
  48.5 38.7 all-gather.2
  89.1 40.5 all-gather.4
where the time goes:
time: 207 us; the launch traced here: 205 us
  waiting for transfers between devices  62.6 us (30%)
  matrix products  36.5 us (18%)
  local copies, waits for them, and re-layouts  30.9 us (15%)
  starting transfers between devices  25.9 us (13%)
  blocking collectives  25.5 us (12%)
  between operations  14.2 us (7%)
  other arithmetic  9.37 us (5%)
    all_gather x1, waiting for transfers between devices, per_device(): lax.all_gather(tile_panel, 'site', axis=0, tiled=True)  42.4 us
    dot_general x8, matrix products, one_group(): jnp.einsum('abrq,bqc->arc', high_part, group_panel, preferred_element_typ...  14.8 us
    unnamed x1, blocking collectives  13.6 us
    dot_general x8, matrix products, one_group(): jnp.einsum('abrq,bqc->arc', low_part, group_panel, preferred_element_type...  13.6 us
    all_to_all x1, blocking collectives, per_device(): lax.all_to_all(send_panel, 'pop', split_axis=0, concat_axis=0, tiled=True)  11.9 us
    all_to_all x1, starting transfers between devices, per_device(): lax.all_to_all(sent_back, 'pop', split_axis=0, concat_axis=0, tiled=True)  11.2 us
    all_to_all x1, starting transfers between devices, per_device(): lax.all_to_all(send_rows, 'pop', split_axis=0, concat_axis=0, tiled=True)  8.59 us
    all_to_all x1, waiting for transfers between devices, per_device(): lax.all_to_all(sent_back, 'pop', split_axis=0, concat_axis=0, tiled=True)  8.32 us
  transfers between devices with their start and end apart: 5, of which 5 were waited for; matrix products, arithmetic and copies ran while one was open for 8% of the time, Pallas kernels for 0%

commit v1 on v0

--- a/solution.py
+++ b/solution.py
@@ -3,6 +3,11 @@
 import jax.numpy as jnp
 from jax import lax
 from jax.sharding import PartitionSpec as P
+
+
+def tiled_gather(x, axis, dim):
+    copies = jnp.concatenate([x] * lax.axis_size(axis), axis=dim)
+    return lax.all_to_all(copies, axis, dim, dim, tiled=True)
 
 
 def pair_terms(own_weights, own_places, running, pieces):
@@ -100,7 +105,7 @@
         initial,
         (
             lax.all_gather(tile_weights, "site", axis=0, tiled=True),
-            lax.all_gather(tile_panel, "site", axis=0, tiled=True),
+            tiled_gather(tile_panel, "site", 0),
             lax.all_gather(tile_loc, "site", axis=0, tiled=True),
         ),
     )

time: 207 us -> 228 us (1.10)
  waiting for transfers between devices: 62.6 us -> 29.5 us
  blocking collectives: 25.5 us -> 53.4 us
  local copies, waits for them, and re-layouts: 30.9 us -> 47.9 us
  starting transfers between devices: 25.9 us -> 33 us
    all_gather x1 -> x0, waiting for transfers between devices: 42.4 us -> none  [per_device(): lax.all_gather(tile_panel, 'site', axis=0, tiled=True)]
    unnamed x1, blocking collectives: 13.6 us -> 53.4 us
    while x0 -> x16, local copies, waits for them, and re-layouts: none -> 15.3 us
    all_to_all x0 -> x2, starting transfers between devices: none -> 12.4 us  [the longest x1 8.19 us: tiled_gather(): return lax.all_to_all(copies, axis, dim, dim, tiled=True)]
    all_to_all x1 -> x0, blocking collectives: 11.9 us -> none  [per_device(): lax.all_to_all(send_panel, 'pop', split_axis=0, concat_axis=0, tiled=True)]
    dot_general x8, matrix products: 14.8 us -> 24.6 us  [one_group(): jnp.einsum('abrq,bqc->arc', high_part, group_panel, preferred_element_typ...]
    dot_general x8, matrix products: 13.6 us -> 5.98 us  [one_group(): jnp.einsum('abrq,bqc->arc', low_part, group_panel, preferred_element_type...]
    all_gather x1, waiting for transfers between devices: 3.46 us -> 9.8 us  [per_device(): lax.all_gather(tile_weights, 'site', axis=0, tiled=True)]
  transfers between devices with their start and end apart: 5 -> 6, of which waited for: 5 -> 5; matrix products, arithmetic and copies ran while one was open for 8% -> 8% of each run, Pallas kernels for 0% -> 0%
where the time goes in v1:
time: 228 us; the launch traced here: 227 us
  blocking collectives  53.4 us (23%)
  local copies, waits for them, and re-layouts  47.9 us (21%)
  matrix products  38.6 us (17%)
  starting transfers between devices  33 us (14%)
  waiting for transfers between devices  29.5 us (13%)
  between operations  14.4 us (6%)
  other arithmetic  10 us (4%)
    unnamed x1, blocking collectives  53.4 us
    dot_general x8, matrix products, one_group(): jnp.einsum('abrq,bqc->arc', high_part, group_panel, preferred_element_typ...  24.6 us
    while x16, local copies, waits for them, and re-layouts  15.3 us
    all_gather x1, waiting for transfers between devices, per_device(): lax.all_gather(tile_weights, 'site', axis=0, tiled=True)  9.8 us
    all_to_all x1, starting transfers between devices, per_device(): lax.all_to_all(send_rows, 'pop', split_axis=0, concat_axis=0, tiled=True)  8.59 us
    all_to_all x1, waiting for transfers between devices, per_device(): lax.all_to_all(sent_back, 'pop', split_axis=0, concat_axis=0, tiled=True)  8.32 us
    all_to_all x1, starting transfers between devices, tiled_gather(): return lax.all_to_all(copies, axis, dim, dim, tiled=True)  8.19 us
    dynamic_slice x16, local copies, waits for them, and re-layouts, pair_terms(): result_sum, unused = lax.scan(one_group, running, grouped)  7.75 us
  transfers between devices with their start and end apart: 6, of which 5 were waited for; matrix products, arithmetic and copies ran while one was open for 8% of the time, Pallas kernels for 0%

profile of v1, /device:TPU:1, one launch (start us, length us, event | category | flops | bytes accessed | tf_op | source)
XLA Modules:
  0.0 227.2 jit_solution(15145794949303971905)
XLA Ops:
  10.1 2.6 %scatter_custom_fusion = s32[768]{0:T(1024)S(1)} fusion(s32[512]{0:T(512)S(1)} %compare_select_fusion.3, s32[512]{0:T(512)} %param.14, s32[]{:T(128)} %constant.8.clone.1), kind=kCustom, calls=%fused_computation.79 | custom fusion | bytes 3584 | tf_op jit(solution)/shard_map/scatter | solution.py:80
  13.4 8.6 %all-to-all-start = ((s32[32,1,24]{2,1,0:T(1,128)}), s32[32,1,24]{2,1,0:T(1,128)S(1)}, u32[]{:S(2)}, u32[]{:S(2)}) async-start(s32[32,1,24]{2,1,0:T(1,128)} %bitcast.2), calls=%async_computation | async-start | bytes 32768 | tf_op jit(solution)/shard_map/all_to_all | solution.py:86
  22.7 6.2 %all-to-all-done = s32[32,1,24]{2,1,0:T(1,128)S(1)} async-done(((s32[32,1,24]{2,1,0:T(1,128)}), s32[32,1,24]{2,1,0:T(1,128)S(1)}, u32[]{:S(2)}, u32[]{:S(2)}) %all-to-all-start) | async-done | bytes 3104 | tf_op jit(solution)/shard_map/all_to_all | solution.py:86
  30.2 3.6 %scatter_custom_fusion.3 = bf16[768,128]{1,0:T(8,128)(2,1)} fusion(s32[512]{0:T(512)S(1)} %compare_select_fusion.3, bf16[128,128]{1,0:T(8,128)(2,1)S(1)} %copy-done, s32[1024]{0:T(1024)S(1)} %get-tuple-element.105, bf16[]{:T(256)} %constant.19.clone.1), kind=kCustom, calls=%fused_computation.41 | custom fusion | bytes 196610 | tf_op jit(solution)/shard_map/scatter | solution.py:74
  33.9 4.2 %all-to-all-start.2 = ((bf16[32,24,128]{2,1,0:T(8,128)(2,1)}), bf16[32,24,128]{2,1,0:T(8,128)(2,1)S(1)}, u32[]{:S(2)}, u32[]{:S(2)}) async-start(bf16[32,24,128]{2,1,0:T(8,128)(2,1)} %bitcast.8), calls=%async_computation.2 | async-start | bytes 393216 | tf_op jit(solution)/shard_map/all_to_all | solution.py:85
  39.7 3.9 %scatter_custom_fusion.1 = bf16[768,96]{1,0:T(8,128)(2,1)} fusion(s32[512]{0:T(512)S(1)} %compare_select_fusion.3, s32[512]{0:T(512)S(1)} %add_minimum_fusion, s32[512]{0:T(512)} %param.15, bf16[]{:T(256)} %constant.19.clone.1, bf16[128,96]{1,0:T(8,128)(2,1)S(1)} %copy.29, s32[1024]{0:T(1024)S(1)} %get-tuple-element.105), kind=kCustom, calls=%fused_computation.40 | custom fusion | flops 196608 | bytes 189440 | tf_op jit(solution)/shard_map/scatter | solution.py:68
  43.6 2.9 %all-to-all-done.2 = bf16[32,24,128]{2,1,0:T(8,128)(2,1)S(1)} async-done(((bf16[32,24,128]{2,1,0:T(8,128)(2,1)}), bf16[32,24,128]{2,1,0:T(8,128)(2,1)S(1)}, u32[]{:S(2)}, u32[]{:S(2)}) %all-to-all-start.2) | async-done | bytes 196640 | tf_op jit(solution)/shard_map/all_to_all | solution.py:85
  46.5 4.7 %all-to-all-start.1 = ((bf16[32,24,96]{2,1,0:T(8,128)(2,1)}), bf16[32,24,96]{2,1,0:T(8,128)(2,1)S(1)}, u32[]{:S(2)}, u32[]{:S(2)}) async-start(bf16[32,24,96]{2,1,0:T(8,128)(2,1)} %bitcast.3), calls=%async_computation.1 | async-start | bytes 393216 | tf_op jit(solution)/shard_map/all_to_all | solution.py:84
  51.1 4.3 %scatter_custom_fusion.4 = bf16[1024,128]{1,0:T(8,128)(2,1)S(1)} fusion(s32[768]{0:T(1024)S(1)} %fusion.39, bf16[768,128]{1,0:T(8,128)(2,1)S(1)} %bitcast.116, bf16[]{:T(256)} %constant.19.clone.1), kind=kCustom, calls=%fused_computation.43 | custom fusion | bytes 262146 | tf_op jit(solution)/shard_map/scatter | solution.py:98
  59.5 8.2 %all-to-all-start.3 = ((bf16[64,128,128]{2,1,0:T(8,128)(2,1)}), bf16[64,128,128]{2,1,0:T(8,128)(2,1)S(1)}, u32[]{:S(2)}, u32[]{:S(2)}) async-start(bf16[64,128,128]{2,1,0:T(8,128)(2,1)} %copy-done.2), calls=%async_computation.3 | async-start | bytes 4194304 | tf_op jit(solution)/shard_map/all_to_all | solution.py:10
  67.9 4.3 %scatter_custom_fusion.2 = bf16[1024,96]{1,0:T(8,128)(2,1)S(1)} fusion(s32[768]{0:T(1024)S(1)} %fusion.39, bf16[768,96]{1,0:T(8,128)(2,1)S(1)} %bitcast.115, bf16[]{:T(256)} %constant.19.clone.1), kind=kCustom, calls=%fused_computation.47 | custom fusion | bytes 196610 | tf_op jit(solution)/shard_map/scatter | solution.py:92
  74.7 53.4 %all-reduce = s32[64]{0:T(128)S(1)} all-reduce(s32[64]{0:T(128)S(1)} %dynamic-update-slice), channel_id=1, replica_groups=mesh['pop'=32,'site'=8] {'site'}, use_global_device_ids=true, to_apply=%add | all-reduce | flops 64 | bytes 512
  128.3 9.8 %all-gather.2.cloned.1.call-done = bf16[64,128,96]{1,0,2:T(8,128)(2,1)} async-done(((bf16[8,128,96]{1,0,2:T(8,128)(2,1)}), bf16[64,128,96]{1,0,2:T(8,128)(2,1)}) %all-gather.2.cloned.1.call-update) | async-done | bytes 1572880 | tf_op jit(solution)/shard_map/all_gather | solution.py:107
  138.1 62.0 %while.11 = (s32[]{:T(128)}, f32[8,128,128]{2,1,0:T(8,128)S(1)}, bf16[8,8,128,96]{2,1,0,3:T(8,128)(2,1)}, s32[8]{0:T(128)S(1)}, s32[8,8]{1,0:T(8,128)S(1)}, /*in...) while((s32[]{:T(128)}, f32[8,128,128]{2,1,0:T(8,128)S(1)}, ...), condition=%wide.region_9.10_spmd.clone, body=%wide.region_8.9_spmd.clone.sunk | while | flops 743571584 | bytes 33161744 | solution.py:41
  142.8 3.1 %fusion.68 = f32[8,128,128]{2,1,0:T(8,128)S(1)} fusion(f32[8,128,128]{2,1,0:T(8,128)S(1)} %fusion.67, f32[8,128,128]{2,1,0:T(8,128)S(1)} %get-tuple-element.159, pred[]{:T(512)S(6)} %compare.3, bf16[8,8,128,128]{3,2,1,0:T(8,128)(2,1)S(1)} %get-tuple-element.173, s32[]{:T(128)} %get-tuple-element.158, f32[8,8,128,128]{3,2,1,0:T(8,128)} %copy-done.1), kind=kOutput, calls=%fused_computation.18.clone.1 | convolution fusion | flops 268828672 | bytes 6029317 | tf_op jit(solution)/shard_map/while/body/eval_jaxpr/abrq,bqc->arc/dot_general | solution.py:33
  150.5 3.1 %fusion.68 = f32[8,128,128]{2,1,0:T(8,128)S(1)} fusion(f32[8,128,128]{2,1,0:T(8,128)S(1)} %fusion.67, f32[8,128,128]{2,1,0:T(8,128)S(1)} %get-tuple-element.159, pred[]{:T(512)S(6)} %compare.3, bf16[8,8,128,128]{3,2,1,0:T(8,128)(2,1)S(1)} %get-tuple-element.173, s32[]{:T(128)} %get-tuple-element.158, f32[8,8,128,128]{3,2,1,0:T(8,128)} %copy-done.1), kind=kOutput, calls=%fused_computation.18.clone.1 | convolution fusion | flops 268828672 | bytes 6029317 | tf_op jit(solution)/shard_map/while/body/eval_jaxpr/abrq,bqc->arc/dot_general | solution.py:33
  158.3 3.1 %fusion.68 = f32[8,128,128]{2,1,0:T(8,128)S(1)} fusion(f32[8,128,128]{2,1,0:T(8,128)S(1)} %fusion.67, f32[8,128,128]{2,1,0:T(8,128)S(1)} %get-tuple-element.159, pred[]{:T(512)S(6)} %compare.3, bf16[8,8,128,128]{3,2,1,0:T(8,128)(2,1)S(1)} %get-tuple-element.173, s32[]{:T(128)} %get-tuple-element.158, f32[8,8,128,128]{3,2,1,0:T(8,128)} %copy-done.1), kind=kOutput, calls=%fused_computation.18.clone.1 | convolution fusion | flops 268828672 | bytes 6029317 | tf_op jit(solution)/shard_map/while/body/eval_jaxpr/abrq,bqc->arc/dot_general | solution.py:33
  166.0 3.1 %fusion.68 = f32[8,128,128]{2,1,0:T(8,128)S(1)} fusion(f32[8,128,128]{2,1,0:T(8,128)S(1)} %fusion.67, f32[8,128,128]{2,1,0:T(8,128)S(1)} %get-tuple-element.159, pred[]{:T(512)S(6)} %compare.3, bf16[8,8,128,128]{3,2,1,0:T(8,128)(2,1)S(1)} %get-tuple-element.173, s32[]{:T(128)} %get-tuple-element.158, f32[8,8,128,128]{3,2,1,0:T(8,128)} %copy-done.1), kind=kOutput, calls=%fused_computation.18.clone.1 | convolution fusion | flops 268828672 | bytes 6029317 | tf_op jit(solution)/shard_map/while/body/eval_jaxpr/abrq,bqc->arc/dot_general | solution.py:33
  173.8 3.1 %fusion.68 = f32[8,128,128]{2,1,0:T(8,128)S(1)} fusion(f32[8,128,128]{2,1,0:T(8,128)S(1)} %fusion.67, f32[8,128,128]{2,1,0:T(8,128)S(1)} %get-tuple-element.159, pred[]{:T(512)S(6)} %compare.3, bf16[8,8,128,128]{3,2,1,0:T(8,128)(2,1)S(1)} %get-tuple-element.173, s32[]{:T(128)} %get-tuple-element.158, f32[8,8,128,128]{3,2,1,0:T(8,128)} %copy-done.1), kind=kOutput, calls=%fused_computation.18.clone.1 | convolution fusion | flops 268828672 | bytes 6029317 | tf_op jit(solution)/shard_map/while/body/eval_jaxpr/abrq,bqc->arc/dot_general | solution.py:33
  181.6 3.1 %fusion.68 = f32[8,128,128]{2,1,0:T(8,128)S(1)} fusion(f32[8,128,128]{2,1,0:T(8,128)S(1)} %fusion.67, f32[8,128,128]{2,1,0:T(8,128)S(1)} %get-tuple-element.159, pred[]{:T(512)S(6)} %compare.3, bf16[8,8,128,128]{3,2,1,0:T(8,128)(2,1)S(1)} %get-tuple-element.173, s32[]{:T(128)} %get-tuple-element.158, f32[8,8,128,128]{3,2,1,0:T(8,128)} %copy-done.1), kind=kOutput, calls=%fused_computation.18.clone.1 | convolution fusion | flops 268828672 | bytes 6029317 | tf_op jit(solution)/shard_map/while/body/eval_jaxpr/abrq,bqc->arc/dot_general | solution.py:33
  189.3 3.1 %fusion.68 = f32[8,128,128]{2,1,0:T(8,128)S(1)} fusion(f32[8,128,128]{2,1,0:T(8,128)S(1)} %fusion.67, f32[8,128,128]{2,1,0:T(8,128)S(1)} %get-tuple-element.159, pred[]{:T(512)S(6)} %compare.3, bf16[8,8,128,128]{3,2,1,0:T(8,128)(2,1)S(1)} %get-tuple-element.173, s32[]{:T(128)} %get-tuple-element.158, f32[8,8,128,128]{3,2,1,0:T(8,128)} %copy-done.1), kind=kOutput, calls=%fused_computation.18.clone.1 | convolution fusion | flops 268828672 | bytes 6029317 | tf_op jit(solution)/shard_map/while/body/eval_jaxpr/abrq,bqc->arc/dot_general | solution.py:33
  197.1 3.1 %fusion.68 = f32[8,128,128]{2,1,0:T(8,128)S(1)} fusion(f32[8,128,128]{2,1,0:T(8,128)S(1)} %fusion.67, f32[8,128,128]{2,1,0:T(8,128)S(1)} %get-tuple-element.159, pred[]{:T(512)S(6)} %compare.3, bf16[8,8,128,128]{3,2,1,0:T(8,128)(2,1)S(1)} %get-tuple-element.173, s32[]{:T(128)} %get-tuple-element.158, f32[8,8,128,128]{3,2,1,0:T(8,128)} %copy-done.1), kind=kOutput, calls=%fused_computation.18.clone.1 | convolution fusion | flops 268828672 | bytes 6029317 | tf_op jit(solution)/shard_map/while/body/eval_jaxpr/abrq,bqc->arc/dot_general | solution.py:33
  202.7 7.1 %all-to-all-start.4 = ((bf16[32,24,128]{2,1,0:T(8,128)(2,1)}), bf16[32,24,128]{2,1,0:T(8,128)(2,1)S(1)}, u32[]{:S(2)}, u32[]{:S(2)}) async-start(bf16[32,24,128]{2,1,0:T(8,128)(2,1)} %bitcast.14), calls=%async_computation.4 | async-start | bytes 393216 | tf_op jit(solution)/shard_map/all_to_all | solution.py:114
  209.9 8.3 %all-to-all-done.4 = bf16[32,24,128]{2,1,0:T(8,128)(2,1)S(1)} async-done(((bf16[32,24,128]{2,1,0:T(8,128)(2,1)}), bf16[32,24,128]{2,1,0:T(8,128)(2,1)S(1)}, u32[]{:S(2)}, u32[]{:S(2)}) %all-to-all-start.4) | async-done | bytes 196640 | tf_op jit(solution)/shard_map/all_to_all | solution.py:114
  (116 shorter events, 55.8 us)
Async XLA Ops:
  6.5 23.7 %copy-start = (bf16[128,128]{1,0:T(8,128)(2,1)S(1)}, bf16[128,128]{1,0:T(8,128)(2,1)}, u32[]{:S(2)}) copy-start(bf16[128,128]{1,0:T(8,128)(2,1)} %param.11) | copy-start | bytes 98308
  13.4 15.5 %all-to-all-start = ((s32[32,1,24]{2,1,0:T(1,128)}), s32[32,1,24]{2,1,0:T(1,128)S(1)}, u32[]{:S(2)}, u32[]{:S(2)}) async-start(s32[32,1,24]{2,1,0:T(1,128)} %bitcast.2), calls=%async_computation | async-start | bytes 32768 | tf_op jit(solution)/shard_map/all_to_all | solution.py:86
  33.9 12.6 %all-to-all-start.2 = ((bf16[32,24,128]{2,1,0:T(8,128)(2,1)}), bf16[32,24,128]{2,1,0:T(8,128)(2,1)S(1)}, u32[]{:S(2)}, u32[]{:S(2)}) async-start(bf16[32,24,128]{2,1,0:T(8,128)(2,1)} %bitcast.8), calls=%async_computation.2 | async-start | bytes 393216 | tf_op jit(solution)/shard_map/all_to_all | solution.py:85
  46.5 13.0 %all-to-all-start.1 = ((bf16[32,24,96]{2,1,0:T(8,128)(2,1)}), bf16[32,24,96]{2,1,0:T(8,128)(2,1)S(1)}, u32[]{:S(2)}, u32[]{:S(2)}) async-start(bf16[32,24,96]{2,1,0:T(8,128)(2,1)} %bitcast.3), calls=%async_computation.1 | async-start | bytes 393216 | tf_op jit(solution)/shard_map/all_to_all | solution.py:84
  55.8 1.4 copy-start.2
  57.1 15.9 %copy-start.5 = (u32[256]{0:T(256)S(1)}, u32[256]{0:T(256)}, u32[]{:S(2)}) copy-start(u32[256]{0:T(256)} %constant.52) | copy-start | bytes 3076
  57.1 17.3 %copy-start.3 = (s32[8]{0:T(128)S(1)}, s32[8]{0:T(128)}, u32[]{:S(2)}) copy-start(s32[8]{0:T(128)} %param.17) | copy-start | bytes 100
  59.5 78.7 %all-to-all-start.3 = ((bf16[64,128,128]{2,1,0:T(8,128)(2,1)}), bf16[64,128,128]{2,1,0:T(8,128)(2,1)S(1)}, u32[]{:S(2)}, u32[]{:S(2)}) async-start(bf16[64,128,128]{2,1,0:T(8,128)(2,1)} %copy-done.2), calls=%async_computation.3 | async-start | bytes 4194304 | tf_op jit(solution)/shard_map/all_to_all | solution.py:10
  67.7 70.5 %all-gather.2.cloned.1.call-start = ((), (), s32[]{:S(2)}) async-start(), calls=%async_computation.5 | async-start | bytes 1769472 | tf_op jit(solution)/shard_map/all_gather | solution.py:107
  140.1 1.9 copy-start.1
  147.9 1.9 copy-start.1
  155.6 1.9 copy-start.1
  163.4 1.9 copy-start.1
  171.1 1.9 copy-start.1
  178.9 1.9 copy-start.1
  186.6 1.9 copy-start.1
  194.4 1.9 copy-start.1
  200.1 19.4 %copy-start.4 = (s32[512]{0:T(512)S(1)}, s32[512]{0:T(512)}, u32[]{:S(2)}) copy-start(s32[512]{0:T(512)} %param.12) | copy-start | bytes 6148
  202.7 15.5 %all-to-all-start.4 = ((bf16[32,24,128]{2,1,0:T(8,128)(2,1)}), bf16[32,24,128]{2,1,0:T(8,128)(2,1)S(1)}, u32[]{:S(2)}, u32[]{:S(2)}) async-start(bf16[32,24,128]{2,1,0:T(8,128)(2,1)} %bitcast.14), calls=%async_computation.4 | async-start | bytes 393216 | tf_op jit(solution)/shard_map/all_to_all | solution.py:114
Sparse Core Ops, SparseCore 0:
  73.2 64.8 all-gather.1
